TPU v7x, 512 devices: a whole 4x8x8 slice. The times are simulated.
512 devices in a mesh: ctx: 64 (over x, y, core), head: 8 (over z).
Axes of the slice: x: 4, y: 8, z: 8, core: 2. Of those that a mesh axis runs over, the one named last changes fastest.
Arguments:
- features: bfloat16 [32768, 8192], P(('ctx', 'head')), may hold values from -6 to 6
- input_map: bfloat16 [32768, 1024], P(('ctx', 'head')), may hold values from -6 to 6
- output_map: bfloat16 [32768, 1024], P(('ctx', 'head')), may hold values from -0.5 to 0.5
- log_decay: float32 [128, 32768], P('head', 'ctx'), may hold values from -2.3 to 0
- step_size: float32 [128, 32768], P('head', 'ctx'), may hold values from 0 to 1.25
- skip_gain: float32 [128], P('head'), may hold values from 0.5 to 2
Outputs:
- mixer_output: bfloat16 [32768, 8192], P(('ctx', 'head'))
All inputs are finite; a program needn't handle non-finite values.
Results may differ from a plain program's by a relative error of at most 0.0043.
Values may be sent and summed in bfloat16 or wider, within the bound.
A program may use at most 128 MiB of HBM per device.

v0:
```python
import jax
import jax.numpy as jnp
from jax import lax
from jax.sharding import PartitionSpec as P

HEAD_DIM = 64
STATE = 128
BLOCK = 256


def prefix(value, axis, combine, identity):
    devices, position = (lax.axis_size(axis), lax.axis_index(axis))
    everything = jax.tree.map(lambda part: lax.all_gather(part, axis), value)
    start = jax.tree.map(
        lambda part, zero: jnp.broadcast_to(jnp.asarray(zero, part.dtype), part.shape),
        value,
        identity,
    )

    def hop(k, before):
        reached = k < position
        new = combine(before, jax.tree.map(lambda part: part[k], everything))
        return jax.tree.map(lambda a, b: jnp.where(reached, a, b), new, before)

    return lax.fori_loop(0, devices, hop, start)


def join(earlier, later):
    return (earlier[0] + later[0], jnp.exp(later[0])[:, None, None] * earlier[1] + later[1])


def carry_in(device_log, closing):
    neutral = (jnp.zeros_like(device_log), jnp.zeros_like(closing))
    whole = prefix((device_log, closing), "ctx", join, neutral)
    return whole[1]


def per_device(features, input_map, output_map, log_decay, step_size, skip_gain):
    features, input_map, output_map = (
        lax.all_to_all(features, "head", split_axis=1, concat_axis=0, tiled=True),
        lax.all_to_all(input_map, "head", split_axis=1, concat_axis=0, tiled=True),
        lax.all_to_all(output_map, "head", split_axis=1, concat_axis=0, tiled=True),
    )
    head_count = log_decay.shape[0]
    length = features.shape[0]
    group_count = input_map.shape[1] // STATE
    per_group = head_count // group_count
    blocks = length // BLOCK
    highest = lax.Precision.HIGHEST
    running_all = jnp.cumsum(log_decay.reshape(head_count, blocks, BLOCK), axis=2)
    steps_all = step_size.reshape(head_count, blocks, BLOCK)
    totals = running_all[:, :, -1]
    rows = lax.broadcasted_iota(jnp.int32, (BLOCK, BLOCK), 0)
    cols = lax.broadcasted_iota(jnp.int32, (BLOCK, BLOCK), 1)
    causal = rows >= cols

    def slab(index):
        lower = index * BLOCK
        slab_in = features[lower : lower + BLOCK].reshape(BLOCK, head_count, HEAD_DIM)
        slab_write = input_map[lower : lower + BLOCK].reshape(BLOCK, group_count, STATE)
        slab_read = output_map[lower : lower + BLOCK].reshape(BLOCK, group_count, STATE)
        return (
            slab_in,
            slab_write,
            slab_read,
            running_all[:, index],
            steps_all[:, index],
            totals[:, index],
        )

    def carried(slab_read, slab_run, state):
        readout = jnp.einsum(
            "tgn,grnp->tgrp",
            slab_read.astype(jnp.float32),
            state.reshape(group_count, per_group, STATE, HEAD_DIM),
            precision=highest,
        )
        return readout.reshape(BLOCK, head_count, HEAD_DIM) * jnp.exp(slab_run).T[:, :, None]

    device_log = jnp.sum(totals, axis=1)
    outputs = []
    state = jnp.zeros((head_count, STATE, HEAD_DIM), jnp.float32)
    for index in range(blocks):
        slab_in, slab_write, slab_read, slab_run, slab_step, slab_total = slab(index)
        affinity = jnp.einsum(
            "tgn,sgn->gts", slab_read, slab_write, preferred_element_type=jnp.float32
        )
        affinity = jnp.repeat(affinity, per_group, axis=0)
        gap = jnp.where(causal[None], slab_run[:, :, None] - slab_run[:, None, :], 0.0)
        decay_table = jnp.where(causal[None], jnp.exp(gap), 0.0)
        weights = (affinity * decay_table * slab_step[:, None, :]).astype(jnp.bfloat16)
        result = jnp.einsum("hts,shp->thp", weights, slab_in, preferred_element_type=jnp.float32)
        if index > 0:
            result = result + carried(slab_read, slab_run, state)
        factor = (jnp.exp(slab_total[:, None] - slab_run) * slab_step).T
        scaled = (slab_in * factor[:, :, None]).astype(jnp.bfloat16)
        fresh = jnp.einsum(
            "tgn,tgrp->grnp",
            slab_write,
            scaled.reshape(BLOCK, group_count, per_group, HEAD_DIM),
            preferred_element_type=jnp.float32,
        )
        state = jnp.exp(slab_total)[:, None, None] * state + fresh.reshape(
            head_count, STATE, HEAD_DIM
        )
        outputs.append(result)
    entering = carry_in(device_log, state)
    offset = jnp.zeros((head_count,), jnp.float32)
    for index in range(blocks):
        slab_in, slab_write, slab_read, slab_run, slab_step, slab_total = slab(index)
        outputs[index] = outputs[index] + carried(slab_read, slab_run + offset[:, None], entering)
        offset = offset + slab_total
    finished = []
    for index in range(blocks):
        slab_in = features[index * BLOCK : (index + 1) * BLOCK].reshape(BLOCK, head_count, HEAD_DIM)
        finished.append(outputs[index] + skip_gain[None, :, None] * slab_in.astype(jnp.float32))
    mixer_output = (
        jnp.concatenate(finished, axis=0)
        .reshape(length, head_count * HEAD_DIM)
        .astype(jnp.bfloat16)
    )
    return lax.all_to_all(mixer_output, "head", split_axis=0, concat_axis=1, tiled=True)


def solution(mesh):
    placed = (
        P(("ctx", "head"), None),
        P(("ctx", "head"), None),
        P(("ctx", "head"), None),
        P("head", "ctx"),
        P("head", "ctx"),
        P("head"),
    )
    return jax.shard_map(
        per_device, mesh=mesh, in_specs=placed, out_specs=P(("ctx", "head"), None), check_vma=False
    )
```

profile of v0, /device:TPU:1, one launch (start us, length us, event | category | flops | bytes accessed | tf_op | source)
XLA Modules:
  0.0 370.1 jit_solution(11832420713626075592)
XLA Ops:
  8.1 10.9 %all-to-all-start.1 = ((bf16[64,8,128]{2,0,1:T(8,128)(2,1)}), bf16[64,8,128]{2,0,1:T(8,128)(2,1)S(1)}, u32[]{:S(2)}, u32[]{:S(2)}) async-start(bf16[64,8,128]{2,0,1:T(8,128)(2,1)} %copy_bitcast_fusion.1), calls=%async_computation.1 | async-start | bytes 262144 | tf_op jit(solution)/shard_map/all_to_all | solution.py:41
  19.0 2.3 copy.123
  21.3 5.5 %all-to-all-done.1 = bf16[64,8,128]{2,0,1:T(8,128)(2,1)S(1)} async-done(((bf16[64,8,128]{2,0,1:T(8,128)(2,1)}), bf16[64,8,128]{2,0,1:T(8,128)(2,1)S(1)}, u32[]{:S(2)}, u32[]{:S(2)}) %all-to-all-start.1) | async-done | bytes 131104 | tf_op jit(solution)/shard_map/all_to_all | solution.py:41
  26.7 3.6 all-to-all-start.2
  30.4 1.2 reduce-window.6
  34.1 1.6 mul.143
  37.1 1.6 mul.148
  39.4 19.9 %all-to-all-done.2 = bf16[64,8,1024]{2,0,1:T(8,128)(2,1)S(1)} async-done(((bf16[64,8,1024]{2,0,1:T(8,128)(2,1)}), bf16[64,8,1024]{2,0,1:T(8,128)(2,1)S(1)}, u32[]{:S(2)}, u32[]{:S(2)}) %all-to-all-start.2) | async-done | bytes 1048608 | tf_op jit(solution)/shard_map/all_to_all | solution.py:40
  59.3 1.9 multiply_convert_fusion.8
  61.3 1.6 convert_element_type.51
  63.6 1.8 fusion.27
  65.3 1.3 fusion.28
  67.4 3.4 all-to-all-start
  70.8 1.3 dynamic-slice
  73.0 127.0 %all-reduce = f32[1024]{0:T(1024)S(1)} all-reduce(f32[1024]{0:T(1024)S(1)} %dynamic-update-slice), channel_id=2, replica_groups=mesh['ctx'=64,'head'=8] {'ctx'}, use_global_device_ids=true, to_apply=%add | all-reduce | flops 1024 | bytes 8192
  204.9 1.8 reshape.172
  206.7 1.6 copy.93
  208.3 3.0 fusion.15
  211.3 1.6 fusion.24
  212.9 2.6 fusion.16
  215.4 109.9 %while.14 = (s32[]{:T(128)}, f32[16,128,64]{2,1,0:T(8,128)S(1)}, s32[]{:T(128)}, f32[64,16]{1,0:T(8,128)S(1)}, f32[64,16,128,64]{2,3,1,0:T(8,128)}, /*index=5*/s32[]{:T(128)}, s32[]{:T(128)}) while((s32[]{:T(128)}, f32[16,128,64]{2,1,0:T(8,128)S(1)}, s32[]{:T(128)}, f32[64,16]{1,0:T(8,128)S(1)}, f32[64,16,128,64]{2,3,1,0:T(8,128)}, ...), condition=%wide.region_4.5_spmd.clone, body=%wide.region_3.4_spmd.clone.sunk | while | flops 524292 | bytes 3670313 | solution.py:25
  215.5 1.1 constant_dynamic-slice_fusion.2
  217.2 1.1 constant_dynamic-slice_fusion.2
  218.9 1.1 constant_dynamic-slice_fusion.2
  225.8 1.1 constant_dynamic-slice_fusion.2
  234.4 1.1 constant_dynamic-slice_fusion.2
  241.2 1.1 constant_dynamic-slice_fusion.2
  242.9 1.1 constant_dynamic-slice_fusion.2
  249.8 1.1 constant_dynamic-slice_fusion.2
  251.5 1.1 constant_dynamic-slice_fusion.2
  258.4 1.1 constant_dynamic-slice_fusion.2
  267.0 1.1 constant_dynamic-slice_fusion.2
  273.8 1.1 constant_dynamic-slice_fusion.2
  275.6 1.1 constant_dynamic-slice_fusion.2
  282.4 1.1 constant_dynamic-slice_fusion.2
  284.1 1.1 constant_dynamic-slice_fusion.2
  291.0 1.1 constant_dynamic-slice_fusion.2
  299.6 1.1 constant_dynamic-slice_fusion.2
  306.4 1.1 constant_dynamic-slice_fusion.2
  308.2 1.1 constant_dynamic-slice_fusion.2
  315.0 1.1 constant_dynamic-slice_fusion.2
  316.7 1.1 constant_dynamic-slice_fusion.2
  323.6 1.1 constant_dynamic-slice_fusion.2
  325.3 2.5 fusion.25
  327.8 2.3 fusion.26
  330.3 1.1 reshape.186
  331.4 1.4 copy.100
  332.8 29.4 %all_to_all.64 = bf16[8,64,1024]{2,1,0:T(8,128)(2,1)S(1)} all-to-all(bf16[8,64,1024]{2,1,0:T(8,128)(2,1)S(1)} %copy.100), channel_id=1, replica_groups=mesh['ctx'=64,'head'=8] {'head'}, dimensions={0} | all-to-all | bytes 2097152 | tf_op jit(solution)/shard_map/all_to_all | solution.py:122
  (305 shorter events, 97.2 us)
Async XLA Ops:
  6.5 0.9 copy-start
  6.5 23.8 %copy-start.10 = (f32[16,512]{1,0:T(8,128)S(1)}, f32[16,512]{1,0:T(8,128)}, u32[]{:S(2)}) copy-start(f32[16,512]{1,0:T(8,128)} %param.11) | copy-start | bytes 98308
  6.5 25.3 %copy-start.11 = (f32[16,512]{1,0:T(8,128)S(1)}, f32[16,512]{1,0:T(8,128)}, u32[]{:S(2)}) copy-start(f32[16,512]{1,0:T(8,128)} %param.12) | copy-start | bytes 98308
  8.1 18.6 %all-to-all-start.1 = ((bf16[64,8,128]{2,0,1:T(8,128)(2,1)}), bf16[64,8,128]{2,0,1:T(8,128)(2,1)S(1)}, u32[]{:S(2)}, u32[]{:S(2)}) async-start(bf16[64,8,128]{2,0,1:T(8,128)(2,1)} %copy_bitcast_fusion.1), calls=%async_computation.1 | async-start | bytes 262144 | tf_op jit(solution)/shard_map/all_to_all | solution.py:41
  26.7 32.6 %all-to-all-start.2 = ((bf16[64,8,1024]{2,0,1:T(8,128)(2,1)}), bf16[64,8,1024]{2,0,1:T(8,128)(2,1)S(1)}, u32[]{:S(2)}, u32[]{:S(2)}) async-start(bf16[64,8,1024]{2,0,1:T(8,128)(2,1)} %bitcast.159), calls=%async_computation.2 | async-start | bytes 2097152 | tf_op jit(solution)/shard_map/all_to_all | solution.py:40
  30.3 185.1 %all-gather.3.cloned.1.call-start = ((), (), s32[]{:S(2)}) async-start(), calls=%async_computation.4 | async-start | bytes 34078720 | tf_op jit(solution)/shard_map/all_gather | solution.py:13
  31.9 1.5 copy-start.1
  32.6 0.8 copy-start.12
  32.7 0.7 copy-start.4
  61.3 5.5 %copy-start.6 = (bf16[64,1024]{1,0:T(8,128)(2,1)S(1)}, bf16[64,1024]{1,0:T(8,128)(2,1)}, u32[]{:S(2)}) copy-start(bf16[64,1024]{1,0:T(8,128)(2,1)} %param.10) | copy-start | bytes 393220
  61.3 11.5 %copy-start.14 = (f32[16]{0:T(128)S(1)}, f32[16]{0:T(128)}, u32[]{:S(2)}) copy-start(f32[16]{0:T(128)} %get-tuple-element.138) | copy-start | bytes 196
  61.3 138.8 %copy-start.2 = (f32[16,2,256]{2,0,1:T(8,128)S(1)}, f32[16,2,256]{2,0,1:T(8,128)}, u32[]{:S(2)}) copy-start(f32[16,2,256]{2,0,1:T(8,128)} %copy-done.1) | copy-start | bytes 98308
  61.3 138.8 %copy-start.5 = (f32[16,1,256]{2,1,0:T(1,128)S(1)}, f32[16,1,256]{2,1,0:T(1,128)}, u32[]{:S(2)}) copy-start(f32[16,1,256]{2,1,0:T(1,128)} %copy-done.4) | copy-start | bytes 49156
  67.4 133.3 %all-to-all-start = ((bf16[64,8,128]{2,0,1:T(8,128)(2,1)}), bf16[64,8,128]{2,0,1:T(8,128)(2,1)S(1)}, u32[]{:S(2)}, u32[]{:S(2)}) async-start(bf16[64,8,128]{2,0,1:T(8,128)(2,1)} %copy_bitcast_fusion.2), calls=%async_computation | async-start | bytes 262144 | tf_op jit(solution)/shard_map/all_to_all | solution.py:42
  208.3 3.0 copy-start.9
  208.3 4.6 %copy-start.3 = (f32[256,256]{1,0:T(8,128)S(1)}, f32[256,256]{1,0:T(8,128)}, u32[]{:S(2)}) copy-start(f32[256,256]{1,0:T(8,128)} %fusion.39) | copy-start | bytes 786436
  215.4 109.9 %copy-start.8 = (f32[256,16]{0,1:T(8,128)S(1)}, f32[256,16]{0,1:T(8,128)}, u32[]{:S(2)}) copy-start(f32[256,16]{0,1:T(8,128)} %get-tuple-element.158) | copy-start | bytes 49156
  215.4 109.9 %copy-start.13 = (f32[16]{0:T(128)S(1)}, f32[16]{0:T(128)}, u32[]{:S(2)}) copy-start(f32[16]{0:T(128)} %param.13) | copy-start | bytes 196
  215.4 112.4 %copy-start.7 = (f32[256,16]{0,1:T(8,128)S(1)}, f32[256,16]{0,1:T(8,128)}, u32[]{:S(2)}) copy-start(f32[256,16]{0,1:T(8,128)} %get-tuple-element.160) | copy-start | bytes 49156
Sparse Core Ops, SparseCore 0:
  66.8 144.3 all-gather.2
where the time goes:
time: 377 us; the launch traced here: 370 us
  blocking collectives  156 us (41%)
  local copies, waits for them, and re-layouts  116 us (31%)
  waiting for transfers between devices  25.5 us (7%)
  other arithmetic  20.9 us (6%)
  starting transfers between devices  17.8 us (5%)
  matrix products  16.8 us (4%)
  between operations  14.4 us (4%)
    unnamed x1, blocking collectives  127 us
    dynamic_slice x128, local copies, waits for them, and re-layouts, hop(): new = combine(before, jax.tree.map(lambda part: part[k], everything))  90.6 us
    all_to_all x1, blocking collectives, per_device(): lax.all_to_all(mixer_output, 'head', split_axis=0, concat_axis=1, tiled=T...  29.4 us
    all_to_all x1, waiting for transfers between devices, per_device(): lax.all_to_all(features, 'head', split_axis=1, concat_axis=0, tiled=True)  19.9 us
    select_n x64, other arithmetic, hop(): return jax.tree.map(lambda a, b: jnp.where(reached, a, b), new, before)  15.5 us
    all_to_all x1, starting transfers between devices, per_device(): lax.all_to_all(input_map, 'head', split_axis=1, concat_axis=0, tiled=True)  10.9 us
  transfers between devices with their start and end apart: 4, of which 2 were waited for; matrix products, arithmetic and copies ran while one was open for 8% of the time, Pallas kernels for 0%

commit v1 on v0

v1 whole, which is shorter than its diff:
```python
import functools

import jax
import jax.numpy as jnp
from jax import lax
from jax.experimental import pallas as pl
from jax.experimental.pallas import tpu as pltpu
from jax.sharding import PartitionSpec as P

HEAD_DIM = 64
STATE = 128
BLOCK = 256
CHUNKS = 4
ROWS = 16
LANES = 128
F32 = jnp.float32
BF16 = jnp.bfloat16
MESH = pl.DeviceIdType.MESH


def kernel(
    nctx, nz,
    feat, bmap, cmap, logd, step, gain,
    out,
    rx, rb, rc, run_row, run_col, fac_col, in_col, out_col, tot, last, aff,
    sbuf, bs0, gath, dg, og, ent, ybuf, obuf,
    x_send, x_recv, b_send, b_recv, c_send, c_recv, d_send, d_recv,
    s_send, s_recv, e_send, e_recv, o_send, o_recv,
):
    ctx = lax.axis_index("ctx")
    z = lax.axis_index("head")
    rows, width = feat.shape[0], feat.shape[1] // nz
    length = rows * nz
    cw = width // CHUNKS
    heads = width // HEAD_DIM
    x_at, y_at, core = ctx // 16, lax.rem(ctx // 2, 8), lax.rem(ctx, 2)
    mine = lax.rem(x_at + y_at, CHUNKS)
    my_rows = pl.ds(pl.multiple_of((x_at * 2 + y_at // 4) * ROWS, ROWS), ROWS)
    my_lanes = pl.ds(pl.multiple_of((mine * 2 + core) * LANES, LANES), LANES)

    def wait(ref, sem):
        pltpu.make_async_copy(ref, ref, sem).wait()

    def send(src, dst, s_sem, r_sem, where):
        pltpu.make_async_remote_copy(
            src_ref=src, dst_ref=dst, send_sem=s_sem, recv_sem=r_sem,
            device_id=where, device_id_type=MESH,
        ).start()

    barrier = pltpu.get_barrier_semaphore()

    def hello_z(d, carry):
        pl.semaphore_signal(barrier, inc=1, device_id={"head": lax.rem(z + d, nz)}, device_id_type=MESH)
        return carry

    def hello_ctx(d, carry):
        pl.semaphore_signal(barrier, inc=1, device_id={"ctx": lax.rem(ctx + d, nctx)}, device_id_type=MESH)
        return carry

    lax.fori_loop(1, nz, hello_z, 0)
    lax.fori_loop(1, nctx, hello_ctx, 0)
    pl.semaphore_wait(barrier, nz + nctx - 2)

    own = pl.ds(pl.multiple_of(z * rows, rows), rows)

    def send_maps(d, carry):
        to = lax.rem(z + d, nz)
        part = pl.ds(pl.multiple_of(to * STATE, STATE), STATE)
        send(bmap.at[:, part], rb.at[own, :], b_send, b_recv, {"head": to})
        send(cmap.at[:, part], rc.at[own, :], c_send, c_recv, {"head": to})
        return carry

    def send_chunk(c):
        def go(d, carry):
            to = lax.rem(z + d, nz)
            part = pl.ds(pl.multiple_of(to * width + c * cw, cw), cw)
            send(feat.at[:, part], rx.at[own, pl.ds(c * cw, cw)], x_send, x_recv.at[c], {"head": to})
            return carry

        lax.fori_loop(1, nz, go, 0)

    lax.fori_loop(1, nz, send_maps, 0)
    for c in range(CHUNKS):
        send_chunk(c)

    rx[own, :] = feat[:, pl.ds(pl.multiple_of(z * width, width), width)]
    rb[own, :] = bmap[:, pl.ds(pl.multiple_of(z * STATE, STATE), STATE)]
    rc[own, :] = cmap[:, pl.ds(pl.multiple_of(z * STATE, STATE), STATE)]

    ti = lax.broadcasted_iota(jnp.int32, (BLOCK, BLOCK), 0)
    si = lax.broadcasted_iota(jnp.int32, (BLOCK, BLOCK), 1)
    upper = jnp.where(ti <= si, 1.0, 0.0).astype(F32)
    closings = []
    for k in range(2):
        at = slice(k * BLOCK, (k + 1) * BLOCK)
        run = jnp.dot(logd[:, at], upper, precision=lax.Precision.HIGHEST, preferred_element_type=F32)
        run_row[:, at] = run
        col = run.T
        run_col[at, :] = col
        closings.append(run[:, BLOCK - 1 : BLOCK])
        closing = col[BLOCK - 1 : BLOCK, :]
        fac_col[at, :] = jnp.exp(closing - col) * step[:, at].T
        in_col[at, :] = jnp.exp(col)
        if k == 0:
            out_col[at, :] = jnp.exp(col)
            first = closing
        else:
            out_col[at, :] = jnp.exp(col + first)
    owner = lax.broadcasted_iota(jnp.int32, (heads, width), 0)
    lane = lax.broadcasted_iota(jnp.int32, (heads, width), 1) // HEAD_DIM

    def spread(column):
        return jnp.sum(jnp.where(owner == lane, column, 0.0), axis=0, keepdims=True)

    last[...] = jnp.broadcast_to(spread(jnp.exp(closings[1])), (8, width))
    tot[...] = jnp.broadcast_to(spread(jnp.exp(closings[0] + closings[1])), (8, width))

    def place(j):
        px, py, pc = j // 16, lax.rem(j // 2, 8), lax.rem(j, 2)
        return lax.rem(px + py, CHUNKS) * 2 + pc

    def send_decay(d, carry):
        to = lax.rem(ctx + d, nctx)
        part = pl.ds(pl.multiple_of(place(to) * LANES, LANES), LANES)
        send(tot.at[:, part], dg.at[ctx], d_send, d_recv, {"ctx": to})
        return carry

    lax.fori_loop(1, nctx, send_decay, 0)
    dg[ctx] = tot[:, my_lanes]

    left = lax.broadcasted_iota(jnp.int32, (BLOCK, LANES), 1) < HEAD_DIM

    def pair_of(ref, at, h):
        return jnp.where(left, ref[at, h : h + 1], ref[at, h + 1 : h + 2])

    def wide(ref, at, c):
        h = c * cw // HEAD_DIM
        return jnp.concatenate([pair_of(ref, at, h + 2 * i) for i in range(cw // LANES)], axis=1)

    n_other = rows * (nz - 1)
    wait(rb.at[pl.ds(0, n_other), :], b_recv)
    wait(rc.at[pl.ds(0, n_other), :], c_recv)
    for k in range(2):
        at = slice(k * BLOCK, (k + 1) * BLOCK)
        aff[at, :] = lax.dot_general(
            rc[at, :], rb[at, :], (((1,), (1,)), ((), ())), preferred_element_type=F32
        )

    def states(c):
        lanes = pl.ds(c * cw, cw)
        wait(rx.at[pl.ds(0, n_other), lanes], x_recv.at[c])
        made = []
        for k in range(2):
            at = slice(k * BLOCK, (k + 1) * BLOCK)
            scaled = (rx[at, lanes].astype(F32) * wide(fac_col, at, c)).astype(BF16)
            made.append(
                lax.dot_general(rb[at, :], scaled, (((0,), (0,)), ((), ())), preferred_element_type=F32)
            )
        sbuf[:, lanes] = (last[0:1, lanes] * made[0] + made[1]).astype(BF16)
        bs0[:, lanes] = made[0].astype(BF16)

        def go(i, carry):
            q = lax.rem(i + ctx, 16)
            tx, th, tc = q // 4, lax.rem(q // 2, 2), lax.rem(q, 2)
            to = tx * 16 + (th * 4 + lax.rem(c - tx + 4, 4)) * 2 + tc

            @pl.when(to != ctx)
            def _():
                send(
                    sbuf.at[
                        pl.ds(pl.multiple_of((tx * 2 + th) * ROWS, ROWS), ROWS),
                        pl.ds(pl.multiple_of((c * 2 + tc) * LANES, LANES), LANES),
                    ],
                    gath.at[ctx], s_send, s_recv, {"ctx": to},
                )

            return carry

        lax.fori_loop(0, 16, go, 0)

    def scan(c):
        @pl.when(mine == c)
        def _():
            gath[ctx] = sbuf[my_rows, my_lanes]
            wait(dg.at[pl.ds(0, nctx - 1)], d_recv)
            wait(gath.at[pl.ds(0, nctx - 1)], s_recv)

            def hop(i, before):
                og[i] = before.astype(BF16)
                decay = dg[i]
                return jnp.concatenate([decay, decay], axis=0) * before + gath[i].astype(F32)

            lax.fori_loop(0, nctx, hop, jnp.zeros((ROWS, LANES), F32))
            ent[my_rows, my_lanes] = og[ctx]

            def go(d, carry):
                to = lax.rem(ctx + d, nctx)
                send(og.at[to], ent.at[my_rows, my_lanes], e_send, e_recv.at[c], {"ctx": to})
                return carry

            lax.fori_loop(1, nctx, go, 0)

    def inside(c):
        def block(k, carry):
            at = pl.ds(pl.multiple_of(k * BLOCK, BLOCK), BLOCK)
            causal = ti >= si
            for i in range(cw // LANES):
                h = c * cw // HEAD_DIM + 2 * i
                lanes = pl.ds(c * cw + i * LANES, LANES)
                xs = rx[at, lanes]
                parts = []
                for j in (h, h + 1):
                    gap = jnp.where(causal, run_col[at, j : j + 1] - run_row[j : j + 1, at], -1e30)
                    weight = (aff[at, :] * jnp.exp(gap) * step[j : j + 1, at]).astype(BF16)
                    parts.append(jnp.dot(weight, xs, preferred_element_type=F32))
                total = jnp.where(left, parts[0], parts[1])
                ybuf[at, lanes] = total + jnp.where(left, gain[h], gain[h + 1]) * xs.astype(F32)

                @pl.when(k == 1)
                def _():
                    read = jnp.dot(rc[at, :], bs0[:, lanes], preferred_element_type=F32)
                    ybuf[at, lanes] += pair_of(in_col, at, h) * read

            return carry

        lax.fori_loop(0, 2, block, 0)

    def finish(c):
        lanes = pl.ds(c * cw, cw)

        @pl.when(mine == c)
        def _():
            wait(og.at[pl.ds(0, 15)], e_recv.at[c])

        @pl.when(mine != c)
        def _():
            wait(og.at[pl.ds(0, 16)], e_recv.at[c])

        for k in range(2):
            at = slice(k * BLOCK, (k + 1) * BLOCK)
            read = jnp.dot(rc[at, :], ent[:, lanes], preferred_element_type=F32)
            obuf[at, lanes] = (ybuf[at, lanes] + wide(out_col, at, c) * read).astype(BF16)
        there = pl.ds(pl.multiple_of(z * width + c * cw, cw), cw)

        def go(d, carry):
            to = lax.rem(z + d, nz)
            send(
                obuf.at[pl.ds(pl.multiple_of(to * rows, rows), rows), lanes],
                out.at[:, there], o_send, o_recv, {"head": to},
            )
            return carry

        lax.fori_loop(1, nz, go, 0)
        out[:, there] = obuf[own, lanes]

    states(0)
    inside(0)
    states(1)
    scan(0)
    inside(1)
    states(2)
    scan(1)
    finish(0)
    inside(2)
    states(3)
    scan(2)
    finish(1)
    inside(3)
    scan(3)
    finish(2)
    finish(3)

    wait(rx.at[pl.ds(0, n_other), :], x_send)
    wait(rb.at[pl.ds(0, n_other), :], b_send)
    wait(rc.at[pl.ds(0, n_other), :], c_send)
    wait(dg.at[pl.ds(0, nctx - 1)], d_send)
    wait(gath.at[pl.ds(0, nctx - 1)], s_send)
    wait(og.at[pl.ds(0, nctx - 1)], e_send)
    wait(obuf.at[pl.ds(0, n_other), :], o_send)
    wait(obuf.at[pl.ds(0, n_other), :], o_recv)


def solution(mesh):
    nctx, nz = mesh.shape["ctx"], mesh.shape["head"]

    def per_device(features, input_map, output_map, log_decay, step_size, skip_gain):
        rows, total = features.shape
        width = total // nz
        length = rows * nz
        heads = width // HEAD_DIM
        vm = pl.BlockSpec(memory_space=pltpu.VMEM)
        dma = pltpu.SemaphoreType.DMA
        return pl.pallas_call(
            functools.partial(kernel, nctx, nz),
            name="mixer",
            out_shape=jax.ShapeDtypeStruct((rows, total), BF16),
            in_specs=[vm, vm, vm, vm, vm, pl.BlockSpec(memory_space=pltpu.SMEM)],
            out_specs=vm,
            scratch_shapes=[
                pltpu.VMEM((length, width), BF16),
                pltpu.VMEM((length, STATE), BF16),
                pltpu.VMEM((length, STATE), BF16),
                pltpu.VMEM((heads, length), F32),
                pltpu.VMEM((length, heads), F32),
                pltpu.VMEM((length, heads), F32),
                pltpu.VMEM((length, heads), F32),
                pltpu.VMEM((length, heads), F32),
                pltpu.VMEM((8, width), F32),
                pltpu.VMEM((8, width), F32),
                pltpu.VMEM((length, BLOCK), F32),
                pltpu.VMEM((STATE, width), BF16),
                pltpu.VMEM((STATE, width), BF16),
                pltpu.VMEM((nctx, ROWS, LANES), BF16),
                pltpu.VMEM((nctx, 8, LANES), F32),
                pltpu.VMEM((nctx, ROWS, LANES), BF16),
                pltpu.VMEM((STATE, width), BF16),
                pltpu.VMEM((length, width), F32),
                pltpu.VMEM((length, width), BF16),
                dma, dma((CHUNKS,)), dma, dma, dma, dma, dma, dma,
                dma, dma, dma, dma((CHUNKS,)), dma, dma,
            ],
            compiler_params=pltpu.CompilerParams(
                collective_id=0, has_side_effects=True, vmem_limit_bytes=40 * 1024 * 1024
            ),
        )(features, input_map, output_map, log_decay, step_size, skip_gain)

    placed = (
        P(("ctx", "head"), None),
        P(("ctx", "head"), None),
        P(("ctx", "head"), None),
        P("head", "ctx"),
        P("head", "ctx"),
        P("head"),
    )
    return jax.shard_map(
        per_device, mesh=mesh, in_specs=placed, out_specs=P(("ctx", "head"), None), check_vma=False
    )
```

time: 377 us -> 79.4 us (0.21); the launches traced: 370 us -> 79 us
  blocking collectives: 156 us -> 0 us
  local copies, waits for them, and re-layouts: 116 us -> 6.17 us
  Pallas kernels: 0 us -> 72.8 us
  waiting for transfers between devices: 25.5 us -> 0 us
  other arithmetic: 20.9 us -> 0 us
  starting transfers between devices: 17.8 us -> 0 us
  matrix products: 16.8 us -> 0 us
  between operations: 14.4 us -> 0.02 us
    unnamed x1 -> x0, blocking collectives: 127 us -> none
    dynamic_slice x128 -> x0, local copies, waits for them, and re-layouts: 90.6 us -> none  [hop(): new = combine(before, jax.tree.map(lambda part: part[k], everything))]
    pallas_call x0 -> x1, Pallas kernels: none -> 72.8 us  [per_device(): pl.pallas_call(functools.partial(kernel, nctx, nz), name='mixer', out_sha...]
    all_to_all x1 -> x0, blocking collectives: 29.4 us -> none  [per_device(): lax.all_to_all(mixer_output, 'head', split_axis=0, concat_axis=1, tiled=T...]
    all_to_all x3 -> x0, waiting for transfers between devices: 25.4 us -> none  [the longest x1 19.9 us: per_device(): lax.all_to_all(features, 'head', split_axis=1, concat_axis=0, tiled=True)]
    all_to_all x3 -> x0, starting transfers between devices: 17.8 us -> none  [the longest x1 10.9 us: per_device(): lax.all_to_all(input_map, 'head', split_axis=1, concat_axis=0, tiled=True)]
    dot_general x9 -> x0, matrix products: 16.8 us -> none  [the longest x3 6.36 us: carried(): jnp.einsum('tgn,grnp->tgrp', slab_read.astype(jnp.float32), state.reshape...]
    select_n x64 -> x0, other arithmetic: 15.5 us -> none  [hop(): return jax.tree.map(lambda a, b: jnp.where(reached, a, b), new, before)]
  transfers between devices with their start and end apart: 4 -> 0, of which waited for: 2 -> 0; matrix products, arithmetic and copies ran while one was open for 8% -> 0% of each run, Pallas kernels for 0% -> 0%
where the time goes in v1:
time: 79.4 us; the launch traced here: 79 us
  Pallas kernels  72.8 us (92%)
  local copies, waits for them, and re-layouts  6.17 us (8%)
    pallas_call x1, Pallas kernels, per_device(): pl.pallas_call(functools.partial(kernel, nctx, nz), name='mixer', out_sha...  72.8 us
    unnamed x13, local copies, waits for them, and re-layouts  6.17 us

profile of v1, /device:TPU:1, one launch (start us, length us, event | category | flops | bytes accessed | tf_op | source)
XLA Modules:
  0.0 79.0 jit_solution(16049547656632188241)
XLA Ops:
  0.0 0.0 copy-start
  0.0 1.2 %copy-done = bf16[64,8192]{1,0:T(8,128)(2,1)S(1)} copy-done((bf16[64,8192]{1,0:T(8,128)(2,1)S(1)}, bf16[64,8192]{1,0:T(8,128)(2,1)}, u32[]{:S(2)}) %copy-start) | copy-done | bytes 1048600
  1.2 0.0 copy-start.1
  1.2 0.9 %copy-done.1 = bf16[64,1024]{1,0:T(8,128)(2,1)S(1)} copy-done((bf16[64,1024]{1,0:T(8,128)(2,1)S(1)}, bf16[64,1024]{1,0:T(8,128)(2,1)}, u32[]{:S(2)}) %copy-start.1) | copy-done | bytes 131096
  2.1 0.0 copy-start.2
  2.1 0.9 %copy-done.2 = bf16[64,1024]{1,0:T(8,128)(2,1)S(1)} copy-done((bf16[64,1024]{1,0:T(8,128)(2,1)S(1)}, bf16[64,1024]{1,0:T(8,128)(2,1)}, u32[]{:S(2)}) %copy-start.2) | copy-done | bytes 131096
  3.0 0.0 copy-start.3
  3.0 0.8 copy-done.3
  3.8 0.0 copy-start.4
  3.8 0.8 copy-done.4
  4.6 0.0 copy-start.5
  4.6 0.7 copy-done.5
  5.2 72.8 %mixer.1 = bf16[64,8192]{1,0:T(8,128)(2,1)S(1)} custom-call(bf16[64,8192]{1,0:T(8,128)(2,1)S(1)} %copy-done, bf16[64,1024]{1,0:T(8,128)(2,1)S(1)} %copy-done.1, bf16[64,1024]{1,0:T(8,128)(2,1)S(1)} %copy-done.2, f32[16,512]{1,0:T(8,128)S(1)} %copy-done.3, f32[16,512]{1,0:T(8,128)S(1)} %copy-done.4, f32[16]{0:T(128)S(1)} %copy-done.5), custom_call_target="tpu_custom_call" | custom-call | tf_op jit(solution)/shard_map/mixer/pallas_call | solution.py:293
  78.0 1.0 %copy.8 = bf16[64,8192]{1,0:T(8,128)(2,1)} copy(bf16[64,8192]{1,0:T(8,128)(2,1)S(1)} %mixer.1) | data formatting | bytes 2097152
Async XLA Ops:
  0.0 1.2 %copy-start = (bf16[64,8192]{1,0:T(8,128)(2,1)S(1)}, bf16[64,8192]{1,0:T(8,128)(2,1)}, u32[]{:S(2)}) copy-start(bf16[64,8192]{1,0:T(8,128)(2,1)} %feat.1) | copy-start | bytes 3145732
  1.2 0.9 %copy-start.1 = (bf16[64,1024]{1,0:T(8,128)(2,1)S(1)}, bf16[64,1024]{1,0:T(8,128)(2,1)}, u32[]{:S(2)}) copy-start(bf16[64,1024]{1,0:T(8,128)(2,1)} %bmap.1) | copy-start | bytes 393220
  2.1 0.9 %copy-start.2 = (bf16[64,1024]{1,0:T(8,128)(2,1)S(1)}, bf16[64,1024]{1,0:T(8,128)(2,1)}, u32[]{:S(2)}) copy-start(bf16[64,1024]{1,0:T(8,128)(2,1)} %cmap.1) | copy-start | bytes 393220
  3.0 0.8 copy-start.3
  3.8 0.8 copy-start.4
  4.6 0.7 copy-start.5

commit v2 on v1

--- a/solution.py
+++ b/solution.py
@@ -20,12 +20,13 @@
 
 def kernel(
     nctx, nz,
-    feat, bmap, cmap, logd, step, gain,
+    feat, bmap, cmap, logd_in, step_in, gain_in,
     out,
+    logd, step, gain, load,
     rx, rb, rc, run_row, run_col, fac_col, in_col, out_col, tot, last, aff,
     sbuf, bs0, gath, dg, og, ent, ybuf, obuf,
     x_send, x_recv, b_send, b_recv, c_send, c_recv, d_send, d_recv,
-    s_send, s_recv, e_send, e_recv, o_send, o_recv,
+    s_send, s_recv, e_send, e_recv, o_send, o_recv, column, ready, keep,
 ):
     ctx = lax.axis_index("ctx")
     z = lax.axis_index("head")
@@ -47,6 +48,23 @@
             device_id=where, device_id_type=MESH,
         ).start()
 
+    def far_first(i):
+        half = (i + 1) // 2
+        return jnp.where(lax.rem(i, 2) == 1, nz // 2 - half, nz // 2 + half)
+
+    own = pl.ds(pl.multiple_of(z * rows, rows), rows)
+
+    def fetch(src, dst, i):
+        copy = pltpu.make_async_copy(src, dst, load.at[i])
+        copy.start()
+        return copy
+
+    small = [fetch(logd_in, logd, 0), fetch(step_in, step, 1), fetch(gain_in, gain, 2)]
+    kept = [
+        fetch(feat.at[:, pl.ds(pl.multiple_of(z * width, width), width)], rx.at[own, :], 3),
+        fetch(bmap.at[:, pl.ds(pl.multiple_of(z * STATE, STATE), STATE)], rb.at[own, :], 4),
+        fetch(cmap.at[:, pl.ds(pl.multiple_of(z * STATE, STATE), STATE)], rc.at[own, :], 5),
+    ]
     barrier = pltpu.get_barrier_semaphore()
 
     def hello_z(d, carry):
@@ -57,14 +75,28 @@
         pl.semaphore_signal(barrier, inc=1, device_id={"ctx": lax.rem(ctx + d, nctx)}, device_id_type=MESH)
         return carry
 
+    def hello_plane(d, carry):
+        pl.semaphore_signal(
+            column, inc=1, device_id={"ctx": lax.rem(ctx + d, nctx)}, device_id_type=MESH
+        )
+        return carry
+
+    def hello_ready(d, carry):
+        pl.semaphore_signal(
+            ready, inc=1, device_id={"head": lax.rem(z + d, nz)}, device_id_type=MESH
+        )
+        return carry
+
     lax.fori_loop(1, nz, hello_z, 0)
-    lax.fori_loop(1, nctx, hello_ctx, 0)
-    pl.semaphore_wait(barrier, nz + nctx - 2)
-
-    own = pl.ds(pl.multiple_of(z * rows, rows), rows)
+
+    @pl.when(z == 0)
+    def _():
+        lax.fori_loop(1, nctx, hello_ctx, 0)
+
+    pl.semaphore_wait(barrier, jnp.where(z == 0, nz + nctx - 2, nz - 1))
 
     def send_maps(d, carry):
-        to = lax.rem(z + d, nz)
+        to = lax.rem(z + far_first(d), nz)
         part = pl.ds(pl.multiple_of(to * STATE, STATE), STATE)
         send(bmap.at[:, part], rb.at[own, :], b_send, b_recv, {"head": to})
         send(cmap.at[:, part], rc.at[own, :], c_send, c_recv, {"head": to})
@@ -72,20 +104,23 @@
 
     def send_chunk(c):
         def go(d, carry):
-            to = lax.rem(z + d, nz)
+            to = lax.rem(z + far_first(d), nz)
             part = pl.ds(pl.multiple_of(to * width + c * cw, cw), cw)
             send(feat.at[:, part], rx.at[own, pl.ds(c * cw, cw)], x_send, x_recv.at[c], {"head": to})
             return carry
 
-        lax.fori_loop(1, nz, go, 0)
-
-    lax.fori_loop(1, nz, send_maps, 0)
+        lax.fori_loop(0, nz - 1, go, 0)
+
+    lax.fori_loop(0, nz - 1, send_maps, 0)
     for c in range(CHUNKS):
         send_chunk(c)
 
-    rx[own, :] = feat[:, pl.ds(pl.multiple_of(z * width, width), width)]
-    rb[own, :] = bmap[:, pl.ds(pl.multiple_of(z * STATE, STATE), STATE)]
-    rc[own, :] = cmap[:, pl.ds(pl.multiple_of(z * STATE, STATE), STATE)]
+    @pl.when(z == 0)
+    def _():
+        lax.fori_loop(1, nctx, hello_plane, 0)
+
+    for copy in small:
+        copy.wait()
 
     ti = lax.broadcasted_iota(jnp.int32, (BLOCK, BLOCK), 0)
     si = lax.broadcasted_iota(jnp.int32, (BLOCK, BLOCK), 1)
@@ -125,7 +160,6 @@
         send(tot.at[:, part], dg.at[ctx], d_send, d_recv, {"ctx": to})
         return carry
 
-    lax.fori_loop(1, nctx, send_decay, 0)
     dg[ctx] = tot[:, my_lanes]
 
     left = lax.broadcasted_iota(jnp.int32, (BLOCK, LANES), 1) < HEAD_DIM
@@ -138,6 +172,8 @@
         return jnp.concatenate([pair_of(ref, at, h + 2 * i) for i in range(cw // LANES)], axis=1)
 
     n_other = rows * (nz - 1)
+    for copy in kept:
+        copy.wait()
     wait(rb.at[pl.ds(0, n_other), :], b_recv)
     wait(rc.at[pl.ds(0, n_other), :], c_recv)
     for k in range(2):
@@ -145,6 +181,17 @@
         aff[at, :] = lax.dot_general(
             rc[at, :], rb[at, :], (((1,), (1,)), ((), ())), preferred_element_type=F32
         )
+
+    @pl.when(z == 0)
+    def _():
+        pl.semaphore_wait(column, nctx - 1)
+        lax.fori_loop(1, nz, hello_ready, 0)
+
+    @pl.when(z != 0)
+    def _():
+        pl.semaphore_wait(ready, 1)
+
+    lax.fori_loop(1, nctx, send_decay, 0)
 
     def states(c):
         lanes = pl.ds(c * cw, cw)
@@ -243,15 +290,15 @@
         there = pl.ds(pl.multiple_of(z * width + c * cw, cw), cw)
 
         def go(d, carry):
-            to = lax.rem(z + d, nz)
+            to = lax.rem(z + far_first(d), nz)
             send(
                 obuf.at[pl.ds(pl.multiple_of(to * rows, rows), rows), lanes],
                 out.at[:, there], o_send, o_recv, {"head": to},
             )
             return carry
 
-        lax.fori_loop(1, nz, go, 0)
-        out[:, there] = obuf[own, lanes]
+        lax.fori_loop(0, nz - 1, go, 0)
+        pltpu.make_async_copy(obuf.at[own, lanes], out.at[:, there], keep).start()
 
     states(0)
     inside(0)
@@ -260,12 +307,12 @@
     inside(1)
     states(2)
     scan(1)
+    inside(2)
     finish(0)
-    inside(2)
     states(3)
     scan(2)
+    inside(3)
     finish(1)
-    inside(3)
     scan(3)
     finish(2)
     finish(3)
@@ -278,6 +325,7 @@
     wait(og.at[pl.ds(0, nctx - 1)], e_send)
     wait(obuf.at[pl.ds(0, n_other), :], o_send)
     wait(obuf.at[pl.ds(0, n_other), :], o_recv)
+    wait(obuf.at[own, :], keep)
 
 
 def solution(mesh):
@@ -294,9 +342,13 @@
             functools.partial(kernel, nctx, nz),
             name="mixer",
             out_shape=jax.ShapeDtypeStruct((rows, total), BF16),
-            in_specs=[vm, vm, vm, vm, vm, pl.BlockSpec(memory_space=pltpu.SMEM)],
-            out_specs=vm,
+            in_specs=[pl.BlockSpec(memory_space=pltpu.HBM)] * 6,
+            out_specs=pl.BlockSpec(memory_space=pltpu.HBM),
             scratch_shapes=[
+                pltpu.VMEM((heads, length), F32),
+                pltpu.VMEM((heads, length), F32),
+                pltpu.SMEM((heads,), F32),
+                dma((6,)),
                 pltpu.VMEM((length, width), BF16),
                 pltpu.VMEM((length, STATE), BF16),
                 pltpu.VMEM((length, STATE), BF16),
@@ -318,9 +370,10 @@
                 pltpu.VMEM((length, width), BF16),
                 dma, dma((CHUNKS,)), dma, dma, dma, dma, dma, dma,
                 dma, dma, dma, dma((CHUNKS,)), dma, dma,
+                pltpu.SemaphoreType.REGULAR, pltpu.SemaphoreType.REGULAR, dma,
             ],
             compiler_params=pltpu.CompilerParams(
-                collective_id=0, has_side_effects=True, vmem_limit_bytes=40 * 1024 * 1024
+                collective_id=0, has_side_effects=True, vmem_limit_bytes=63 * 1024 * 1024
             ),
         )(features, input_map, output_map, log_decay, step_size, skip_gain)
 

time: 79.4 us -> 72.5 us (0.913)
  local copies, waits for them, and re-layouts: 6.17 us -> 2.26 us
  Pallas kernels: 72.8 us -> 69.5 us
    unnamed x13 -> x1, local copies, waits for them, and re-layouts: 6.17 us -> 2.26 us
    pallas_call x1, Pallas kernels: 72.8 us -> 69.5 us  [per_device(): pl.pallas_call(functools.partial(kernel, nctx, nz), name='mixer', out_sha...]
where the time goes in v2:
time: 72.5 us; the launch traced here: 71.7 us
  Pallas kernels  69.5 us (96%)
  local copies, waits for them, and re-layouts  2.26 us (3%)
    pallas_call x1, Pallas kernels, per_device(): pl.pallas_call(functools.partial(kernel, nctx, nz), name='mixer', out_sha...  69.5 us
    unnamed x1, local copies, waits for them, and re-layouts  2.26 us

profile of v2, /device:TPU:1, one launch (start us, length us, event | category | flops | bytes accessed | tf_op | source)
XLA Modules:
  0.0 71.7 jit_solution(201682887990841632)
XLA Ops:
  0.0 69.5 %mixer.1 = bf16[64,8192]{1,0:T(8,128)(2,1)} custom-call(bf16[64,8192]{1,0:T(8,128)(2,1)} %feat.1, bf16[64,1024]{1,0:T(8,128)(2,1)} %bmap.1, bf16[64,1024]{1,0:T(8,128)(2,1)} %cmap.1, f32[16,512]{1,0:T(8,128)} %logd_in.1, f32[16,512]{1,0:T(8,128)} %step_in.1, f32[16]{0:T(128)} %gain_in.1), custom_call_target="tpu_custom_call" | custom-call | tf_op jit(solution)/shard_map/mixer/pallas_call | solution.py:341
  69.5 2.3 %copy.8 = bf16[64,8192]{1,0:T(8,128)(2,1)} copy(bf16[64,8192]{1,0:T(8,128)(2,1)} %mixer.1) | data formatting | bytes 2097152

commit v3 on v2

--- a/solution.py
+++ b/solution.py
@@ -10,7 +10,7 @@
 HEAD_DIM = 64
 STATE = 128
 BLOCK = 256
-CHUNKS = 4
+CHUNKS = 8
 ROWS = 16
 LANES = 128
 F32 = jnp.float32
@@ -35,9 +35,9 @@
     cw = width // CHUNKS
     heads = width // HEAD_DIM
     x_at, y_at, core = ctx // 16, lax.rem(ctx // 2, 8), lax.rem(ctx, 2)
-    mine = lax.rem(x_at + y_at, CHUNKS)
+    mine = lax.rem(x_at + y_at, 4) * 2 + core
     my_rows = pl.ds(pl.multiple_of((x_at * 2 + y_at // 4) * ROWS, ROWS), ROWS)
-    my_lanes = pl.ds(pl.multiple_of((mine * 2 + core) * LANES, LANES), LANES)
+    my_lanes = pl.ds(pl.multiple_of(mine * LANES, LANES), LANES)
 
     def wait(ref, sem):
         pltpu.make_async_copy(ref, ref, sem).wait()
@@ -152,7 +152,7 @@
 
     def place(j):
         px, py, pc = j // 16, lax.rem(j // 2, 8), lax.rem(j, 2)
-        return lax.rem(px + py, CHUNKS) * 2 + pc
+        return lax.rem(px + py, 4) * 2 + pc
 
     def send_decay(d, carry):
         to = lax.rem(ctx + d, nctx)
@@ -207,23 +207,23 @@
         bs0[:, lanes] = made[0].astype(BF16)
 
         def go(i, carry):
-            q = lax.rem(i + ctx, 16)
-            tx, th, tc = q // 4, lax.rem(q // 2, 2), lax.rem(q, 2)
-            to = tx * 16 + (th * 4 + lax.rem(c - tx + 4, 4)) * 2 + tc
+            q = lax.rem(i + ctx, 8)
+            tx, th = q // 2, lax.rem(q, 2)
+            to = tx * 16 + (th * 4 + lax.rem(c // 2 - tx + 4, 4)) * 2 + c % 2
 
             @pl.when(to != ctx)
             def _():
                 send(
                     sbuf.at[
                         pl.ds(pl.multiple_of((tx * 2 + th) * ROWS, ROWS), ROWS),
-                        pl.ds(pl.multiple_of((c * 2 + tc) * LANES, LANES), LANES),
+                        pl.ds(c * LANES, LANES),
                     ],
                     gath.at[ctx], s_send, s_recv, {"ctx": to},
                 )
 
             return carry
 
-        lax.fori_loop(0, 16, go, 0)
+        lax.fori_loop(0, 8, go, 0)
 
     def scan(c):
         @pl.when(mine == c)
@@ -277,11 +277,11 @@
 
         @pl.when(mine == c)
         def _():
-            wait(og.at[pl.ds(0, 15)], e_recv.at[c])
+            wait(og.at[pl.ds(0, 7)], e_recv.at[c])
 
         @pl.when(mine != c)
         def _():
-            wait(og.at[pl.ds(0, 16)], e_recv.at[c])
+            wait(og.at[pl.ds(0, 8)], e_recv.at[c])
 
         for k in range(2):
             at = slice(k * BLOCK, (k + 1) * BLOCK)
@@ -303,19 +303,35 @@
     states(0)
     inside(0)
     states(1)
-    scan(0)
     inside(1)
     states(2)
+    scan(0)
+    inside(2)
+    states(3)
     scan(1)
-    inside(2)
+    inside(3)
+    states(4)
+    scan(2)
+    inside(4)
     finish(0)
-    states(3)
-    scan(2)
-    inside(3)
+    states(5)
+    scan(3)
+    inside(5)
     finish(1)
-    scan(3)
+    states(6)
+    scan(4)
+    inside(6)
     finish(2)
+    states(7)
+    scan(5)
+    inside(7)
     finish(3)
+    scan(6)
+    finish(4)
+    scan(7)
+    finish(5)
+    finish(6)
+    finish(7)
 
     wait(rx.at[pl.ds(0, n_other), :], x_send)
     wait(rb.at[pl.ds(0, n_other), :], b_send)

time: 72.5 us -> 71.2 us (0.982)
  no operation moved by 1% of the time
where the time goes in v3:
time: 71.2 us; the launch traced here: 71.1 us
  Pallas kernels  68.8 us (97%)
  local copies, waits for them, and re-layouts  2.26 us (3%)
    pallas_call x1, Pallas kernels, per_device(): pl.pallas_call(functools.partial(kernel, nctx, nz), name='mixer', out_sha...  68.8 us
    unnamed x1, local copies, waits for them, and re-layouts  2.26 us

profile of v3, /device:TPU:1, one launch (start us, length us, event | category | flops | bytes accessed | tf_op | source)
XLA Modules:
  0.0 71.1 jit_solution(7560298637158077229)
XLA Ops:
  0.0 68.8 %mixer.1 = bf16[64,8192]{1,0:T(8,128)(2,1)} custom-call(bf16[64,8192]{1,0:T(8,128)(2,1)} %feat.1, bf16[64,1024]{1,0:T(8,128)(2,1)} %bmap.1, bf16[64,1024]{1,0:T(8,128)(2,1)} %cmap.1, f32[16,512]{1,0:T(8,128)} %logd_in.1, f32[16,512]{1,0:T(8,128)} %step_in.1, f32[16]{0:T(128)} %gain_in.1), custom_call_target="tpu_custom_call" | custom-call | tf_op jit(solution)/shard_map/mixer/pallas_call | solution.py:357
  68.8 2.3 %copy.8 = bf16[64,8192]{1,0:T(8,128)(2,1)} copy(bf16[64,8192]{1,0:T(8,128)(2,1)} %mixer.1) | data formatting | bytes 2097152
